TPU v7x, 256 devices: a whole 4x4x8 slice. The times are simulated.
256 devices in a mesh: seq: 32 (over x_hi, z, core), batch: 8 (over x_lo, y).
Axes of the slice: x: 4 (x_hi: 2, x_lo: 2; x = x_hi * 2 + x_lo), y: 4, z: 8, core: 2. Of those that a mesh axis runs over, the one named last changes fastest.
Arguments:
- bases: int32 [65536, 128], P(('batch', 'seq')), parts along dimension 0, may hold values from 0 to 3
- embed_table: bfloat16 [512, 768], replicated, may hold values from -0.5 to 0.5
- norm_gains: float32 [3, 768], replicated, may hold values from 0.1 to 1.9
- depth_taps: float32 [3, 5, 768], replicated, may hold values from -2.5 to 2.5
- point_weight: bfloat16 [3, 768, 768], replicated, may hold values from -0.21875 to 0.21875
- query_weight: bfloat16 [768, 128], replicated, may hold values from -0.5390625 to 0.5390625
- key_weight: bfloat16 [768, 128], replicated, may hold values from -0.5390625 to 0.5390625
- pair_kernel: bfloat16 [3, 3, 128, 128], replicated, may hold values from -0.1875 to 0.1875
Outputs:
- trunk: bfloat16 [65536, 768], P(('batch', 'seq')), parts along dimension 0
- pair_map: bfloat16 [4096, 512, 128], P(('batch', 'seq')), parts along dimension 0
There are 8 independent parts, one for each index of `batch`. A program takes and returns all parts, laid end to end along the dimension named above; an argument that names none is the same for every part. Nothing has to cross between parts.
All inputs are finite; a program needn't handle non-finite values.
Results may differ from a plain program's by a relative error of at most 0.018.
Values may be sent and summed in bfloat16 or wider, within the bound.
No kernel may reach another device: no remote copies, remote signals or barrier semaphores. Data moves between devices by JAX's collectives and lax.ppermute only.
A program may use at most 64 MiB of HBM per device.

v0:
```python
import jax
import jax.numpy as jnp
from jax import lax
from jax.sharding import PartitionSpec as P

KW = 5
FIRST_DILATION = 2
SECOND_DILATION = 8
THIRD_DILATION = 32
POOL = 16


def with_halo(cells, sides, width):
    for axis, dim in sides:
        count = lax.axis_size(axis)
        ends = count - 1
        head = lax.slice_in_dim(cells, 0, width, axis=dim)
        tail = lax.slice_in_dim(cells, cells.shape[dim] - width, cells.shape[dim], axis=dim)
        cells = jnp.concatenate(
            [
                lax.ppermute(tail, axis, [(i, (i + 1) % count) for i in range(ends)]),
                cells,
                lax.ppermute(head, axis, [((i + 1) % count, i) for i in range(ends)]),
            ],
            axis=dim,
        )
    return cells


def embed_bases(bases, embed_table):
    one_hot_bases = (bases[:, :, None] == jnp.arange(4, dtype=jnp.int32)).astype(jnp.bfloat16)
    one_hot_bases = one_hot_bases.reshape(bases.shape[0], -1)
    return jnp.dot(one_hot_bases, embed_table, preferred_element_type=jnp.float32).astype(
        jnp.bfloat16
    )


def normalize(value_rows, gain):
    floats = value_rows.astype(jnp.float32)
    scale = lax.rsqrt(jnp.mean(floats * floats, axis=-1, keepdims=True) + 1e-06)
    return (floats * scale * gain).astype(jnp.bfloat16)


def mix_rows(inner, normed, taps, point, dilation_reach, rows):
    summed = jnp.zeros((rows, normed.shape[1]), jnp.float32)
    for offset in range(KW):
        summed = (
            summed
            + normed[offset * dilation_reach : offset * dilation_reach + rows].astype(jnp.float32)
            * taps[offset]
        )
    activated = jax.nn.gelu(summed).astype(jnp.bfloat16)
    return (
        inner.astype(jnp.float32) + jnp.dot(activated, point, preferred_element_type=jnp.float32)
    ).astype(jnp.bfloat16)


def pair_conv(extended, pair_kernel, rows, width):
    padded = jnp.pad(extended, ((0, 0), (1, 1), (0, 0)))
    channels = extended.shape[2]
    summed = jnp.zeros((rows * width, channels), jnp.float32)
    for row_tap in range(3):
        for col_tap in range(3):
            window = padded[row_tap : row_tap + rows, col_tap : col_tap + width].reshape(
                rows * width, channels
            )
            summed = summed + jnp.dot(
                window, pair_kernel[row_tap, col_tap], preferred_element_type=jnp.float32
            )
    center = extended[1 : rows + 1].astype(jnp.float32).reshape(rows * width, channels)
    return (center + jax.nn.gelu(summed)).astype(jnp.bfloat16).reshape(rows, width, channels)


def on_device(
    bases, embed_table, norm_gains, depth_taps, point_weight, query_weight, key_weight, pair_kernel
):
    dilation_reaches = (FIRST_DILATION, SECOND_DILATION, THIRD_DILATION)
    current = embed_bases(bases, embed_table)
    slab_rows = current.shape[0]
    for trunk_layer in range(3):
        dilation_reach = dilation_reaches[trunk_layer]
        normed = normalize(current, norm_gains[trunk_layer])
        widened = with_halo(normed, (("seq", 0),), 2 * dilation_reach)
        current = mix_rows(
            current,
            widened,
            depth_taps[trunk_layer],
            point_weight[trunk_layer],
            dilation_reach,
            slab_rows,
        )
    pooled = jnp.mean(
        current.astype(jnp.float32).reshape(-1, POOL, current.shape[1]), axis=1
    ).astype(jnp.bfloat16)
    queries = jnp.dot(pooled, query_weight, preferred_element_type=jnp.float32).astype(jnp.bfloat16)
    all_keys = jnp.dot(
        lax.all_gather(pooled, "seq", axis=0, tiled=True),
        key_weight,
        preferred_element_type=jnp.float32,
    ).astype(jnp.bfloat16)
    key_floats = all_keys.astype(jnp.float32)[None, :, :]
    pair_rows = queries.shape[0]
    pair = (queries.astype(jnp.float32)[:, None, :] * key_floats).astype(jnp.bfloat16)
    extended = with_halo(pair, (("seq", 0),), 1)
    pair_map = pair_conv(extended, pair_kernel, pair_rows, all_keys.shape[0])
    return (current, pair_map)


def solution(mesh):
    return jax.shard_map(
        on_device,
        mesh=mesh,
        in_specs=(P(("batch", "seq"), None), P(), P(), P(), P(), P(), P(), P()),
        out_specs=(P(("batch", "seq"), None), P(("batch", "seq"), None, None)),
        check_vma=False,
    )
```

profile of v0, /device:TPU:14, one launch (start us, length us, event | category | flops | bytes accessed | tf_op | source)
XLA Modules:
  0.0 109.2 jit_solution(7016129010796559855)
XLA Ops:
  0.6 0.0 copy-start
  0.6 0.8 slice_reduce_fusion.5
  1.5 0.1 eq.23
  1.6 1.0 copy.10
  2.6 0.0 copy-start.5
  2.6 0.1 eq.20
  2.7 0.2 eq.21
  2.9 0.7 multiply_reduce_fusion.2
  3.6 0.1 multiply_convert_fusion.3
  3.8 1.9 %collective-permute-start = (bf16[4,768]{1,0:T(4,128)(2,1)S(1)}, bf16[4,768]{1,0:T(4,128)(2,1)S(1)}, u32[]{:S(2)}, u32[]{:S(2)}) collective-permute-start(bf16[4,768]{1,0:T(4,128)(2,1)S(1)} %get-tuple-element.34), channel_id=1, source_target_pairs={{0,8},{8,16},{16,24},{24,32},{32,40},{40,48},{48,56},{56,64},{64,7... | collective-permute-start | bytes 18440 | tf_op jit(solution)/shard_map/ppermute | solution.py:21
  5.7 8.0 %collective-permute-start.1 = (bf16[4,768]{1,0:T(4,128)(2,1)S(1)}, bf16[4,768]{1,0:T(4,128)(2,1)S(1)}, u32[]{:S(2)}, u32[]{:S(2)}) collective-permute-start(bf16[4,768]{1,0:T(4,128)(2,1)S(1)} %get-tuple-element.35), channel_id=1, source_target_pairs={{8,0},{16,8},{24,16},{32,24},{40,32},{48,40},{56,48},{64,56},{72,6... | collective-permute-start | bytes 18440 | tf_op jit(solution)/shard_map/ppermute | solution.py:23
  13.8 0.1 slice_reduce_fusion.4
  13.9 0.0 collective-permute-done
  13.9 1.2 %collective-permute-done.1 = bf16[4,768]{1,0:T(4,128)(2,1)S(1)} collective-permute-done((bf16[4,768]{1,0:T(4,128)(2,1)S(1)}, bf16[4,768]{1,0:T(4,128)(2,1)S(1)}, u32[]{:S(2)}, u32[]{:S(2)}) %collective-permute-start.1) | collective-permute-done | bytes 6176 | tf_op jit(solution)/shard_map/ppermute | solution.py:23
  15.1 2.6 %multiply_reduce_fusion.1 = (f32[256]{0:T(256)S(1)}, f32[256,768]{1,0:T(8,128)S(1)}) fusion(f32[256,768]{1,0:T(8,128)S(1)} %get-tuple-element.37, bf16[3,768,768]{2,1,0:T(8,128)(2,1)} %param.12, bf16[256,768]{1,0:T(8,128)(2,1)S(1)} %multiply_convert_fusion.3, bf16[4,768]{1,0:T(4,128)(2,1)S(1)} %collective-permute-done.1, ...), kind=kOutput, calls=%fused_computation.80 | convolution fusion | flops 309853952 | bytes 3174400 | tf_op jit(solution)/shard_map/dot_general | solution.py:54
  17.7 0.1 multiply_convert_fusion.2
  17.9 1.9 %collective-permute-start.2 = (bf16[16,768]{1,0:T(8,128)(2,1)S(1)}, bf16[16,768]{1,0:T(8,128)(2,1)S(1)}, u32[]{:S(2)}, u32[]{:S(2)}) collective-permute-start(bf16[16,768]{1,0:T(8,128)(2,1)S(1)} %get-tuple-element.32), channel_id=1, source_target_pairs={{0,8},{8,16},{16,24},{24,32},{32,40},{40,48},{48,56},{56,64},{64,7... | collective-permute-start | bytes 73736 | tf_op jit(solution)/shard_map/ppermute | solution.py:21
  19.8 7.3 %collective-permute-start.3 = (bf16[16,768]{1,0:T(8,128)(2,1)S(1)}, bf16[16,768]{1,0:T(8,128)(2,1)S(1)}, u32[]{:S(2)}, u32[]{:S(2)}) collective-permute-start(bf16[16,768]{1,0:T(8,128)(2,1)S(1)} %get-tuple-element.33), channel_id=1, source_target_pairs={{8,0},{16,8},{24,16},{32,24},{40,32},{48,40},{56,48},{64,56},{72,6... | collective-permute-start | bytes 73736 | tf_op jit(solution)/shard_map/ppermute | solution.py:23
  27.1 1.5 %collective-permute-done.3 = bf16[16,768]{1,0:T(8,128)(2,1)S(1)} collective-permute-done((bf16[16,768]{1,0:T(8,128)(2,1)S(1)}, bf16[16,768]{1,0:T(8,128)(2,1)S(1)}, u32[]{:S(2)}, u32[]{:S(2)}) %collective-permute-start.3) | collective-permute-done | bytes 24608 | tf_op jit(solution)/shard_map/ppermute | solution.py:23
  28.6 1.0 multiply_reduce_fusion
  29.5 0.1 multiply_convert_fusion.1
  29.7 1.9 %collective-permute-start.4 = (bf16[64,768]{1,0:T(8,128)(2,1)S(1)}, bf16[64,768]{1,0:T(8,128)(2,1)S(1)}, u32[]{:S(2)}, u32[]{:S(2)}) collective-permute-start(bf16[64,768]{1,0:T(8,128)(2,1)S(1)} %get-tuple-element.30), channel_id=1, source_target_pairs={{0,8},{8,16},{16,24},{24,32},{32,40},{40,48},{48,56},{56,64},{64,7... | collective-permute-start | bytes 294920 | tf_op jit(solution)/shard_map/ppermute | solution.py:21
  31.6 7.3 %collective-permute-start.5 = (bf16[64,768]{1,0:T(8,128)(2,1)S(1)}, bf16[64,768]{1,0:T(8,128)(2,1)S(1)}, u32[]{:S(2)}, u32[]{:S(2)}) collective-permute-start(bf16[64,768]{1,0:T(8,128)(2,1)S(1)} %get-tuple-element.31), channel_id=1, source_target_pairs={{8,0},{16,8},{24,16},{32,24},{40,32},{48,40},{56,48},{64,56},{72,6... | collective-permute-start | bytes 294920 | tf_op jit(solution)/shard_map/ppermute | solution.py:23
  38.9 0.4 collective-permute-done.4
  39.3 1.8 %collective-permute-done.5 = bf16[64,768]{1,0:T(8,128)(2,1)S(1)} collective-permute-done((bf16[64,768]{1,0:T(8,128)(2,1)S(1)}, bf16[64,768]{1,0:T(8,128)(2,1)S(1)}, u32[]{:S(2)}, u32[]{:S(2)}) %collective-permute-start.5) | collective-permute-done | bytes 98336 | tf_op jit(solution)/shard_map/ppermute | solution.py:23
  41.1 1.8 %convert_reduce_fusion = (f32[16,768]{1,0:T(8,128)S(1)}, bf16[256,768]{1,0:T(8,128)(2,1)}) fusion(f32[256,768]{1,0:T(8,128)S(1)} %get-tuple-element.41, bf16[3,768,768]{2,1,0:T(8,128)(2,1)S(1)} %copy-done.6, bf16[256,768]{1,0:T(8,128)(2,1)S(1)} %multiply_convert_fusion.1, bf16[64,768]{1,0:T(8,128)(2,1)S(1)} %collective-permute-done.5, ...), kind=kOutput, calls=%fused_computation.76 | convolution fusion | flops 309645312 | bytes 3018752 | tf_op jit(solution)/shard_map/dot_general | solution.py:54
  42.9 39.0 %all_gather.3 = bf16[512,768]{1,0:T(8,128)(2,1)S(1)} all-gather(bf16[16,768]{1,0:T(8,128)(2,1)S(1)} %multiply_convert_fusion.4), channel_id=1, replica_groups=mesh['seq'=32,'batch'=8] {'seq'}, dimensions={0}, use_global_device_ids=true | all-gather | bytes 811008 | tf_op jit(solution)/shard_map/all_gather | solution.py:97
  81.9 0.1 fusion.29
  82.0 0.4 fusion.28
  82.4 0.5 multiply_convert_fusion
  82.9 2.3 %collective-permute-start.6 = (bf16[1,512,128]{2,1,0:T(8,128)(2,1)S(1)}, bf16[1,512,128]{2,1,0:T(8,128)(2,1)S(1)}, u32[]{:S(2)}, u32[]{:S(2)}) collective-permute-start(bf16[1,512,128]{2,1,0:T(8,128)(2,1)S(1)} %get-tuple-element.28), channel_id=1, source_target_pairs={{0,8},{8,16},{16,24},{24,32},{32,40},{40,48},{48,56},{56,64},{64,7... | collective-permute-start | bytes 393224 | tf_op jit(solution)/shard_map/ppermute | solution.py:21
  85.2 7.1 %collective-permute-start.7 = (bf16[1,512,128]{2,1,0:T(8,128)(2,1)S(1)}, bf16[1,512,128]{2,1,0:T(8,128)(2,1)S(1)}, u32[]{:S(2)}, u32[]{:S(2)}) collective-permute-start(bf16[1,512,128]{2,1,0:T(8,128)(2,1)S(1)} %get-tuple-element.29), channel_id=1, source_target_pairs={{8,0},{16,8},{24,16},{32,24},{40,32},{48,40},{56,48},{64,56},{72,6... | collective-permute-start | bytes 393224 | tf_op jit(solution)/shard_map/ppermute | solution.py:23
  92.3 0.5 collective-permute-done.6
  92.8 1.8 %collective-permute-done.7 = bf16[1,512,128]{2,1,0:T(8,128)(2,1)S(1)} collective-permute-done((bf16[1,512,128]{2,1,0:T(8,128)(2,1)S(1)}, bf16[1,512,128]{2,1,0:T(8,128)(2,1)S(1)}, u32[]{:S(2)}, u32[]{:S(2)}) %collective-permute-start.7) | collective-permute-done | bytes 131104 | tf_op jit(solution)/shard_map/ppermute | solution.py:23
  94.6 1.4 %fusion.15 = bf16[18,514,128]{2,1,0:T(8,128)(2,1)S(1)} fusion(bf16[1,512,128]{2,1,0:T(8,128)(2,1)S(1)} %collective-permute-done.7, bf16[16,512,128]{2,1,0:T(8,128)(2,1)S(1)} %multiply_convert_fusion, bf16[1,512,128]{2,1,0:T(8,128)(2,1)S(1)} %collective-permute-done.6), kind=kLoop, calls=%fused_computation.26 | loop fusion | flops 14211072 | bytes 4727808 | tf_op jit(solution)/shard_map/concatenate | solution.py:19
  96.1 0.0 copy-start.2
  96.1 3.8 %fusion.133 = (bf16[16,512,128]{2,1,0:T(8,128)(2,1)S(1)}, bf16[16,512,128]{2,1,0:T(8,128)(2,1)S(1)}, bf16[16,512,128]{2,1,0:T(8,128)(2,1)S(1)}, bf16[16,512,128]...) fusion(bf16[18,514,128]{2,1,0:T(8,128)(2,1)S(1)} %fusion.15), kind=kLoop, calls=%fused_computation.199 | loop fusion | bytes 25165824 | tf_op jit(solution)/shard_map/slice | solution.py:64
  99.9 0.7 fusion.107
  100.6 0.7 fusion.98
  101.3 0.4 pad_maximum_fusion
  101.6 0.7 convolution_add_fusion.6
  102.3 0.7 convolution_add_fusion.5
  103.0 0.7 convolution_add_fusion.4
  103.7 0.7 convolution_add_fusion.3
  104.4 0.7 convolution_add_fusion.2
  105.1 0.7 convolution_add_fusion.1
  105.8 0.0 copy-start.1
  105.8 3.3 %fusion.10 = bf16[8192,128]{1,0:T(8,128)(2,1)} fusion(f32[8192,128]{1,0:T(8,128)S(1)} %fusion.98, f32[8192,128]{1,0:T(8,128)S(1)} %convolution_add_fusion.1, bf16[8192,128]{1,0:T(8,128)(2,1)S(1)} %bitcast.80, bf16[8192,128]{1,0:T(8,128)(2,1)S(1)} %bitcast.72, bf16[3,3,128,128]{3,2,1,0:T(8,128)(2,1)S(1)} %copy-done.2), kind=kOutput, calls=%fused_computation.20 | convolution fusion | flops 282066944 | bytes 14712832 | tf_op jit(solution)/shard_map/dot_general | solution.py:67
  (20 shorter events, 0.1 us)
Async XLA Ops:
  0.6 2.3 %copy-start = (bf16[512,768]{1,0:T(8,128)(2,1)S(1)}, bf16[512,768]{1,0:T(8,128)(2,1)}, u32[]{:S(2)}) copy-start(bf16[512,768]{1,0:T(8,128)(2,1)} %param.9) | copy-start | bytes 2359300
  2.6 11.1 %copy-start.5 = (f32[3,5,768]{2,0,1:T(4,128)S(1)}, f32[3,5,768]{2,0,1:T(4,128)}, u32[]{:S(2)}) copy-start(f32[3,5,768]{2,0,1:T(4,128)} %param.11) | copy-start | bytes 138244
  3.8 10.1 %collective-permute-start = (bf16[4,768]{1,0:T(4,128)(2,1)S(1)}, bf16[4,768]{1,0:T(4,128)(2,1)S(1)}, u32[]{:S(2)}, u32[]{:S(2)}) collective-permute-start(bf16[4,768]{1,0:T(4,128)(2,1)S(1)} %get-tuple-element.34), channel_id=1, source_target_pairs={{0,8},{8,16},{16,24},{24,32},{32,40},{40,48},{48,56},{56,64},{64,7... | collective-permute-start | bytes 18440 | tf_op jit(solution)/shard_map/ppermute | solution.py:21
  5.7 9.4 %collective-permute-start.1 = (bf16[4,768]{1,0:T(4,128)(2,1)S(1)}, bf16[4,768]{1,0:T(4,128)(2,1)S(1)}, u32[]{:S(2)}, u32[]{:S(2)}) collective-permute-start(bf16[4,768]{1,0:T(4,128)(2,1)S(1)} %get-tuple-element.35), channel_id=1, source_target_pairs={{8,0},{16,8},{24,16},{32,24},{40,32},{48,40},{56,48},{64,56},{72,6... | collective-permute-start | bytes 18440 | tf_op jit(solution)/shard_map/ppermute | solution.py:23
  15.1 13.4 %copy-start.6 = (bf16[3,768,768]{2,1,0:T(8,128)(2,1)S(1)}, bf16[3,768,768]{2,1,0:T(8,128)(2,1)}, u32[]{:S(2)}) copy-start(bf16[3,768,768]{2,1,0:T(8,128)(2,1)} %param.12) | copy-start | bytes 10616836
  17.9 9.2 %collective-permute-start.2 = (bf16[16,768]{1,0:T(8,128)(2,1)S(1)}, bf16[16,768]{1,0:T(8,128)(2,1)S(1)}, u32[]{:S(2)}, u32[]{:S(2)}) collective-permute-start(bf16[16,768]{1,0:T(8,128)(2,1)S(1)} %get-tuple-element.32), channel_id=1, source_target_pairs={{0,8},{8,16},{16,24},{24,32},{32,40},{40,48},{48,56},{56,64},{64,7... | collective-permute-start | bytes 73736 | tf_op jit(solution)/shard_map/ppermute | solution.py:21
  19.8 8.8 %collective-permute-start.3 = (bf16[16,768]{1,0:T(8,128)(2,1)S(1)}, bf16[16,768]{1,0:T(8,128)(2,1)S(1)}, u32[]{:S(2)}, u32[]{:S(2)}) collective-permute-start(bf16[16,768]{1,0:T(8,128)(2,1)S(1)} %get-tuple-element.33), channel_id=1, source_target_pairs={{8,0},{16,8},{24,16},{32,24},{40,32},{48,40},{56,48},{64,56},{72,6... | collective-permute-start | bytes 73736 | tf_op jit(solution)/shard_map/ppermute | solution.py:23
  29.7 9.6 %collective-permute-start.4 = (bf16[64,768]{1,0:T(8,128)(2,1)S(1)}, bf16[64,768]{1,0:T(8,128)(2,1)S(1)}, u32[]{:S(2)}, u32[]{:S(2)}) collective-permute-start(bf16[64,768]{1,0:T(8,128)(2,1)S(1)} %get-tuple-element.30), channel_id=1, source_target_pairs={{0,8},{8,16},{16,24},{24,32},{32,40},{40,48},{48,56},{56,64},{64,7... | collective-permute-start | bytes 294920 | tf_op jit(solution)/shard_map/ppermute | solution.py:21
  31.6 9.5 %collective-permute-start.5 = (bf16[64,768]{1,0:T(8,128)(2,1)S(1)}, bf16[64,768]{1,0:T(8,128)(2,1)S(1)}, u32[]{:S(2)}, u32[]{:S(2)}) collective-permute-start(bf16[64,768]{1,0:T(8,128)(2,1)S(1)} %get-tuple-element.31), channel_id=1, source_target_pairs={{8,0},{16,8},{24,16},{32,24},{40,32},{48,40},{56,48},{64,56},{72,6... | collective-permute-start | bytes 294920 | tf_op jit(solution)/shard_map/ppermute | solution.py:23
  41.1 40.8 %copy-start.4 = (bf16[768,128]{1,0:T(8,128)(2,1)S(1)}, bf16[768,128]{1,0:T(8,128)(2,1)}, u32[]{:S(2)}) copy-start(bf16[768,128]{1,0:T(8,128)(2,1)} %param.13) | copy-start | bytes 589828
  41.1 40.9 %copy-start.3 = (bf16[768,128]{1,0:T(8,128)(2,1)S(1)}, bf16[768,128]{1,0:T(8,128)(2,1)}, u32[]{:S(2)}) copy-start(bf16[768,128]{1,0:T(8,128)(2,1)} %param.14) | copy-start | bytes 589828
  82.9 9.9 %collective-permute-start.6 = (bf16[1,512,128]{2,1,0:T(8,128)(2,1)S(1)}, bf16[1,512,128]{2,1,0:T(8,128)(2,1)S(1)}, u32[]{:S(2)}, u32[]{:S(2)}) collective-permute-start(bf16[1,512,128]{2,1,0:T(8,128)(2,1)S(1)} %get-tuple-element.28), channel_id=1, source_target_pairs={{0,8},{8,16},{16,24},{24,32},{32,40},{40,48},{48,56},{56,64},{64,7... | collective-permute-start | bytes 393224 | tf_op jit(solution)/shard_map/ppermute | solution.py:21
  85.2 9.4 %collective-permute-start.7 = (bf16[1,512,128]{2,1,0:T(8,128)(2,1)S(1)}, bf16[1,512,128]{2,1,0:T(8,128)(2,1)S(1)}, u32[]{:S(2)}, u32[]{:S(2)}) collective-permute-start(bf16[1,512,128]{2,1,0:T(8,128)(2,1)S(1)} %get-tuple-element.29), channel_id=1, source_target_pairs={{8,0},{16,8},{24,16},{32,24},{40,32},{48,40},{56,48},{64,56},{72,6... | collective-permute-start | bytes 393224 | tf_op jit(solution)/shard_map/ppermute | solution.py:23
  96.1 3.8 %copy-start.2 = (bf16[3,3,128,128]{3,2,1,0:T(8,128)(2,1)S(1)}, bf16[3,3,128,128]{3,2,1,0:T(8,128)(2,1)}, u32[]{:S(2)}) copy-start(bf16[3,3,128,128]{3,2,1,0:T(8,128)(2,1)} %param.15) | copy-start | bytes 884740
  105.8 3.3 %copy-start.1 = (bf16[512,768]{1,0:T(8,128)(2,1)S(1)}, bf16[512,768]{1,0:T(8,128)(2,1)}, u32[]{:S(2)}) copy-start(bf16[512,768]{1,0:T(8,128)(2,1)} %param.9) | copy-start | bytes 2359300
where the time goes:
time: 110 us; the launch traced here: 109 us
  blocking collectives  39 us (35%)
  starting transfers between devices  37.7 us (34%)
  matrix products  15.4 us (14%)
  waiting for transfers between devices  7.18 us (7%)
  local copies, waits for them, and re-layouts  6.22 us (6%)
  other arithmetic  2.74 us (2%)
    all_gather x1, blocking collectives, on_device(): lax.all_gather(pooled, 'seq', axis=0, tiled=True)  39 us
    ppermute x4, starting transfers between devices, with_halo(): lax.ppermute(head, axis, [((i + 1) % count, i) for i in range(ends)])  29.7 us
    dot_general x9, matrix products, pair_conv(): jnp.dot(window, pair_kernel[row_tap, col_tap], preferred_element_type=jnp...  8.85 us
    ppermute x4, starting transfers between devices, with_halo(): lax.ppermute(tail, axis, [(i, (i + 1) % count) for i in range(ends)])  8.02 us
    ppermute x4, waiting for transfers between devices, with_halo(): lax.ppermute(head, axis, [((i + 1) % count, i) for i in range(ends)])  6.28 us
    dot_general x3, matrix products, mix_rows(): jnp.dot(activated, point, preferred_element_type=jnp.float32)  5.33 us
    slice x1, local copies, waits for them, and re-layouts, pair_conv(): padded[row_tap:row_tap + rows, col_tap:col_tap + width]  3.77 us
  transfers between devices with their start and end apart: 8, of which 6 were waited for; matrix products, arithmetic and copies ran while one was open for 0% of the time, Pallas kernels for 0%

commit v1 on v0

--- a/solution.py
+++ b/solution.py
@@ -94,7 +94,9 @@
     ).astype(jnp.bfloat16)
     queries = jnp.dot(pooled, query_weight, preferred_element_type=jnp.float32).astype(jnp.bfloat16)
     all_keys = jnp.dot(
-        lax.all_gather(pooled, "seq", axis=0, tiled=True),
+        jnp.concatenate(
+            lax.all_to_all(jnp.stack([pooled] * lax.axis_size("seq")), "seq", 0, 0), axis=0
+        ),
         key_weight,
         preferred_element_type=jnp.float32,
     ).astype(jnp.bfloat16)

time: 110 us -> 102 us (0.927)
  blocking collectives: 39 us -> 0 us
  waiting for transfers between devices: 7.18 us -> 29.4 us
  starting transfers between devices: 37.7 us -> 45.1 us
    all_gather x1 -> x0, blocking collectives: 39 us -> none  [on_device(): lax.all_gather(pooled, 'seq', axis=0, tiled=True)]
    all_to_all x0 -> x1, waiting for transfers between devices: none -> 22.2 us  [on_device(): lax.all_to_all(jnp.stack([pooled] * lax.axis_size('seq')), 'seq', 0, 0)]
    all_to_all x0 -> x1, starting transfers between devices: none -> 7.44 us  [on_device(): lax.all_to_all(jnp.stack([pooled] * lax.axis_size('seq')), 'seq', 0, 0)]
  transfers between devices with their start and end apart: 8 -> 9, of which waited for: 6 -> 7; matrix products, arithmetic and copies ran while one was open for 0% -> 0% of each run, Pallas kernels for 0% -> 0%
where the time goes in v1:
time: 102 us; the launch traced here: 101 us
  starting transfers between devices  45.1 us (44%)
  waiting for transfers between devices  29.4 us (29%)
  matrix products  15.3 us (15%)
  local copies, waits for them, and re-layouts  7.15 us (7%)
  other arithmetic  2.74 us (3%)
    ppermute x4, starting transfers between devices, with_halo(): lax.ppermute(head, axis, [((i + 1) % count, i) for i in range(ends)])  30 us
    all_to_all x1, waiting for transfers between devices, on_device(): lax.all_to_all(jnp.stack([pooled] * lax.axis_size('seq')), 'seq', 0, 0)  22.2 us
    dot_general x9, matrix products, pair_conv(): jnp.dot(window, pair_kernel[row_tap, col_tap], preferred_element_type=jnp...  8.83 us
    ppermute x4, starting transfers between devices, with_halo(): lax.ppermute(tail, axis, [(i, (i + 1) % count) for i in range(ends)])  7.68 us
    all_to_all x1, starting transfers between devices, on_device(): lax.all_to_all(jnp.stack([pooled] * lax.axis_size('seq')), 'seq', 0, 0)  7.44 us
    ppermute x4, waiting for transfers between devices, with_halo(): lax.ppermute(head, axis, [((i + 1) % count, i) for i in range(ends)])  6.28 us
    dot_general x3, matrix products, mix_rows(): jnp.dot(activated, point, preferred_element_type=jnp.float32)  5.33 us
    slice x1, local copies, waits for them, and re-layouts, pair_conv(): padded[row_tap:row_tap + rows, col_tap:col_tap + width]  3.77 us
  transfers between devices with their start and end apart: 9, of which 7 were waited for; matrix products, arithmetic and copies ran while one was open for 0% of the time, Pallas kernels for 0%

profile of v1, /device:TPU:14, one launch (start us, length us, event | category | flops | bytes accessed | tf_op | source)
XLA Modules:
  0.0 100.7 jit_solution(4892779338536649351)
XLA Ops:
  0.6 0.0 copy-start
  0.6 0.8 slice_reduce_fusion.5
  1.5 0.1 eq.23
  1.6 1.0 copy.10
  2.6 0.0 copy-start.5
  2.6 0.1 eq.20
  2.7 0.2 eq.21
  2.9 0.7 multiply_reduce_fusion.2
  3.6 0.1 multiply_convert_fusion.3
  3.8 1.9 %collective-permute-start = (bf16[4,768]{1,0:T(4,128)(2,1)S(1)}, bf16[4,768]{1,0:T(4,128)(2,1)S(1)}, u32[]{:S(2)}, u32[]{:S(2)}) collective-permute-start(bf16[4,768]{1,0:T(4,128)(2,1)S(1)} %get-tuple-element.34), channel_id=1, source_target_pairs={{0,8},{8,16},{16,24},{24,32},{32,40},{40,48},{48,56},{56,64},{64,7... | collective-permute-start | bytes 18440 | tf_op jit(solution)/shard_map/ppermute | solution.py:21
  5.7 8.0 %collective-permute-start.1 = (bf16[4,768]{1,0:T(4,128)(2,1)S(1)}, bf16[4,768]{1,0:T(4,128)(2,1)S(1)}, u32[]{:S(2)}, u32[]{:S(2)}) collective-permute-start(bf16[4,768]{1,0:T(4,128)(2,1)S(1)} %get-tuple-element.35), channel_id=1, source_target_pairs={{8,0},{16,8},{24,16},{32,24},{40,32},{48,40},{56,48},{64,56},{72,6... | collective-permute-start | bytes 18440 | tf_op jit(solution)/shard_map/ppermute | solution.py:23
  13.8 0.1 slice_reduce_fusion.4
  13.9 1.2 %collective-permute-done.1 = bf16[4,768]{1,0:T(4,128)(2,1)S(1)} collective-permute-done((bf16[4,768]{1,0:T(4,128)(2,1)S(1)}, bf16[4,768]{1,0:T(4,128)(2,1)S(1)}, u32[]{:S(2)}, u32[]{:S(2)}) %collective-permute-start.1) | collective-permute-done | bytes 6176 | tf_op jit(solution)/shard_map/ppermute | solution.py:23
  15.1 2.6 %multiply_reduce_fusion.1 = (f32[256]{0:T(256)S(1)}, f32[256,768]{1,0:T(8,128)S(1)}) fusion(f32[256,768]{1,0:T(8,128)S(1)} %get-tuple-element.37, bf16[3,768,768]{2,1,0:T(8,128)(2,1)} %param.12, bf16[256,768]{1,0:T(8,128)(2,1)S(1)} %multiply_convert_fusion.3, bf16[4,768]{1,0:T(4,128)(2,1)S(1)} %collective-permute-done.1, ...), kind=kOutput, calls=%fused_computation.80 | convolution fusion | flops 309853952 | bytes 3174400 | tf_op jit(solution)/shard_map/dot_general | solution.py:54
  17.7 0.1 multiply_convert_fusion.2
  17.9 1.9 %collective-permute-start.2 = (bf16[16,768]{1,0:T(8,128)(2,1)S(1)}, bf16[16,768]{1,0:T(8,128)(2,1)S(1)}, u32[]{:S(2)}, u32[]{:S(2)}) collective-permute-start(bf16[16,768]{1,0:T(8,128)(2,1)S(1)} %get-tuple-element.32), channel_id=1, source_target_pairs={{0,8},{8,16},{16,24},{24,32},{32,40},{40,48},{48,56},{56,64},{64,7... | collective-permute-start | bytes 73736 | tf_op jit(solution)/shard_map/ppermute | solution.py:21
  19.8 7.3 %collective-permute-start.3 = (bf16[16,768]{1,0:T(8,128)(2,1)S(1)}, bf16[16,768]{1,0:T(8,128)(2,1)S(1)}, u32[]{:S(2)}, u32[]{:S(2)}) collective-permute-start(bf16[16,768]{1,0:T(8,128)(2,1)S(1)} %get-tuple-element.33), channel_id=1, source_target_pairs={{8,0},{16,8},{24,16},{32,24},{40,32},{48,40},{56,48},{64,56},{72,6... | collective-permute-start | bytes 73736 | tf_op jit(solution)/shard_map/ppermute | solution.py:23
  27.1 1.5 %collective-permute-done.3 = bf16[16,768]{1,0:T(8,128)(2,1)S(1)} collective-permute-done((bf16[16,768]{1,0:T(8,128)(2,1)S(1)}, bf16[16,768]{1,0:T(8,128)(2,1)S(1)}, u32[]{:S(2)}, u32[]{:S(2)}) %collective-permute-start.3) | collective-permute-done | bytes 24608 | tf_op jit(solution)/shard_map/ppermute | solution.py:23
  28.6 1.0 multiply_reduce_fusion
  29.5 0.1 multiply_convert_fusion.1
  29.7 1.9 %collective-permute-start.4 = (bf16[64,768]{1,0:T(8,128)(2,1)S(1)}, bf16[64,768]{1,0:T(8,128)(2,1)S(1)}, u32[]{:S(2)}, u32[]{:S(2)}) collective-permute-start(bf16[64,768]{1,0:T(8,128)(2,1)S(1)} %get-tuple-element.30), channel_id=1, source_target_pairs={{0,8},{8,16},{16,24},{24,32},{32,40},{40,48},{48,56},{56,64},{64,7... | collective-permute-start | bytes 294920 | tf_op jit(solution)/shard_map/ppermute | solution.py:21
  31.6 7.3 %collective-permute-start.5 = (bf16[64,768]{1,0:T(8,128)(2,1)S(1)}, bf16[64,768]{1,0:T(8,128)(2,1)S(1)}, u32[]{:S(2)}, u32[]{:S(2)}) collective-permute-start(bf16[64,768]{1,0:T(8,128)(2,1)S(1)} %get-tuple-element.31), channel_id=1, source_target_pairs={{8,0},{16,8},{24,16},{32,24},{40,32},{48,40},{56,48},{64,56},{72,6... | collective-permute-start | bytes 294920 | tf_op jit(solution)/shard_map/ppermute | solution.py:23
  38.9 0.4 collective-permute-done.4
  39.3 1.8 %collective-permute-done.5 = bf16[64,768]{1,0:T(8,128)(2,1)S(1)} collective-permute-done((bf16[64,768]{1,0:T(8,128)(2,1)S(1)}, bf16[64,768]{1,0:T(8,128)(2,1)S(1)}, u32[]{:S(2)}, u32[]{:S(2)}) %collective-permute-start.5) | collective-permute-done | bytes 98336 | tf_op jit(solution)/shard_map/ppermute | solution.py:23
  41.1 1.8 %convert_reduce_fusion = (f32[16,768]{1,0:T(8,128)S(1)}, bf16[256,768]{1,0:T(8,128)(2,1)}) fusion(f32[256,768]{1,0:T(8,128)S(1)} %get-tuple-element.41, bf16[3,768,768]{2,1,0:T(8,128)(2,1)S(1)} %copy-done.6, bf16[256,768]{1,0:T(8,128)(2,1)S(1)} %multiply_convert_fusion.1, bf16[64,768]{1,0:T(8,128)(2,1)S(1)} %collective-permute-done.5, ...), kind=kOutput, calls=%fused_computation.76 | convolution fusion | flops 309645312 | bytes 3018752 | tf_op jit(solution)/shard_map/dot_general | solution.py:54
  42.9 0.9 stack.2
  43.8 7.4 %all-to-all-start = ((bf16[32,16,768]{2,1,0:T(8,128)(2,1)}), bf16[32,16,768]{2,1,0:T(8,128)(2,1)S(1)}, u32[]{:S(2)}, u32[]{:S(2)}) async-start(bf16[32,16,768]{2,1,0:T(8,128)(2,1)} %stack.2), calls=%async_computation | async-start | bytes 1572864 | tf_op jit(solution)/shard_map/all_to_all | solution.py:98
  51.3 0.1 fusion.29
  51.4 22.2 %all-to-all-done = bf16[32,16,768]{2,1,0:T(8,128)(2,1)S(1)} async-done(((bf16[32,16,768]{2,1,0:T(8,128)(2,1)}), bf16[32,16,768]{2,1,0:T(8,128)(2,1)S(1)}, u32[]{:S(2)}, u32[]{:S(2)}) %all-to-all-start) | async-done | bytes 786464 | tf_op jit(solution)/shard_map/all_to_all | solution.py:98
  73.6 0.4 fusion.28
  74.0 0.5 multiply_convert_fusion
  74.5 1.9 %collective-permute-start.6 = (bf16[1,512,128]{2,1,0:T(8,128)(2,1)S(1)}, bf16[1,512,128]{2,1,0:T(8,128)(2,1)S(1)}, u32[]{:S(2)}, u32[]{:S(2)}) collective-permute-start(bf16[1,512,128]{2,1,0:T(8,128)(2,1)S(1)} %get-tuple-element.28), channel_id=1, source_target_pairs={{0,8},{8,16},{16,24},{24,32},{32,40},{40,48},{48,56},{56,64},{64,7... | collective-permute-start | bytes 393224 | tf_op jit(solution)/shard_map/ppermute | solution.py:21
  76.4 7.4 %collective-permute-start.7 = (bf16[1,512,128]{2,1,0:T(8,128)(2,1)S(1)}, bf16[1,512,128]{2,1,0:T(8,128)(2,1)S(1)}, u32[]{:S(2)}, u32[]{:S(2)}) collective-permute-start(bf16[1,512,128]{2,1,0:T(8,128)(2,1)S(1)} %get-tuple-element.29), channel_id=1, source_target_pairs={{8,0},{16,8},{24,16},{32,24},{40,32},{48,40},{56,48},{64,56},{72,6... | collective-permute-start | bytes 393224 | tf_op jit(solution)/shard_map/ppermute | solution.py:23
  83.9 0.5 collective-permute-done.6
  84.4 1.8 %collective-permute-done.7 = bf16[1,512,128]{2,1,0:T(8,128)(2,1)S(1)} collective-permute-done((bf16[1,512,128]{2,1,0:T(8,128)(2,1)S(1)}, bf16[1,512,128]{2,1,0:T(8,128)(2,1)S(1)}, u32[]{:S(2)}, u32[]{:S(2)}) %collective-permute-start.7) | collective-permute-done | bytes 131104 | tf_op jit(solution)/shard_map/ppermute | solution.py:23
  86.2 1.4 %fusion.15 = bf16[18,514,128]{2,1,0:T(8,128)(2,1)S(1)} fusion(bf16[1,512,128]{2,1,0:T(8,128)(2,1)S(1)} %collective-permute-done.7, bf16[16,512,128]{2,1,0:T(8,128)(2,1)S(1)} %multiply_convert_fusion, bf16[1,512,128]{2,1,0:T(8,128)(2,1)S(1)} %collective-permute-done.6), kind=kLoop, calls=%fused_computation.26 | loop fusion | flops 14211072 | bytes 4727808 | tf_op jit(solution)/shard_map/concatenate | solution.py:19
  87.6 0.0 copy-start.2
  87.6 3.8 %fusion.133 = (bf16[16,512,128]{2,1,0:T(8,128)(2,1)S(1)}, bf16[16,512,128]{2,1,0:T(8,128)(2,1)S(1)}, bf16[16,512,128]{2,1,0:T(8,128)(2,1)S(1)}, bf16[16,512,128]...) fusion(bf16[18,514,128]{2,1,0:T(8,128)(2,1)S(1)} %fusion.15), kind=kLoop, calls=%fused_computation.199 | loop fusion | bytes 25165824 | tf_op jit(solution)/shard_map/slice | solution.py:64
  91.4 0.7 fusion.107
  92.1 0.7 fusion.98
  92.8 0.4 pad_maximum_fusion
  93.2 0.7 convolution_add_fusion.6
  93.9 0.7 convolution_add_fusion.5
  94.6 0.7 convolution_add_fusion.4
  95.3 0.7 convolution_add_fusion.3
  95.9 0.7 convolution_add_fusion.2
  96.6 0.7 convolution_add_fusion.1
  97.4 3.3 %fusion.10 = bf16[8192,128]{1,0:T(8,128)(2,1)} fusion(f32[8192,128]{1,0:T(8,128)S(1)} %fusion.98, f32[8192,128]{1,0:T(8,128)S(1)} %convolution_add_fusion.1, bf16[8192,128]{1,0:T(8,128)(2,1)S(1)} %bitcast.82, bf16[8192,128]{1,0:T(8,128)(2,1)S(1)} %bitcast.73, bf16[3,3,128,128]{3,2,1,0:T(8,128)(2,1)S(1)} %copy-done.2), kind=kOutput, calls=%fused_computation.20 | convolution fusion | flops 282066944 | bytes 14712832 | tf_op jit(solution)/shard_map/dot_general | solution.py:67
  (22 shorter events, 0.1 us)
Async XLA Ops:
  0.6 2.3 %copy-start = (bf16[512,768]{1,0:T(8,128)(2,1)S(1)}, bf16[512,768]{1,0:T(8,128)(2,1)}, u32[]{:S(2)}) copy-start(bf16[512,768]{1,0:T(8,128)(2,1)} %param.9) | copy-start | bytes 2359300
  2.6 11.1 %copy-start.5 = (f32[3,5,768]{2,0,1:T(4,128)S(1)}, f32[3,5,768]{2,0,1:T(4,128)}, u32[]{:S(2)}) copy-start(f32[3,5,768]{2,0,1:T(4,128)} %param.11) | copy-start | bytes 138244
  3.8 10.1 %collective-permute-start = (bf16[4,768]{1,0:T(4,128)(2,1)S(1)}, bf16[4,768]{1,0:T(4,128)(2,1)S(1)}, u32[]{:S(2)}, u32[]{:S(2)}) collective-permute-start(bf16[4,768]{1,0:T(4,128)(2,1)S(1)} %get-tuple-element.34), channel_id=1, source_target_pairs={{0,8},{8,16},{16,24},{24,32},{32,40},{40,48},{48,56},{56,64},{64,7... | collective-permute-start | bytes 18440 | tf_op jit(solution)/shard_map/ppermute | solution.py:21
  5.7 9.4 %collective-permute-start.1 = (bf16[4,768]{1,0:T(4,128)(2,1)S(1)}, bf16[4,768]{1,0:T(4,128)(2,1)S(1)}, u32[]{:S(2)}, u32[]{:S(2)}) collective-permute-start(bf16[4,768]{1,0:T(4,128)(2,1)S(1)} %get-tuple-element.35), channel_id=1, source_target_pairs={{8,0},{16,8},{24,16},{32,24},{40,32},{48,40},{56,48},{64,56},{72,6... | collective-permute-start | bytes 18440 | tf_op jit(solution)/shard_map/ppermute | solution.py:23
  15.1 13.4 %copy-start.6 = (bf16[3,768,768]{2,1,0:T(8,128)(2,1)S(1)}, bf16[3,768,768]{2,1,0:T(8,128)(2,1)}, u32[]{:S(2)}) copy-start(bf16[3,768,768]{2,1,0:T(8,128)(2,1)} %param.12) | copy-start | bytes 10616836
  17.9 9.2 %collective-permute-start.2 = (bf16[16,768]{1,0:T(8,128)(2,1)S(1)}, bf16[16,768]{1,0:T(8,128)(2,1)S(1)}, u32[]{:S(2)}, u32[]{:S(2)}) collective-permute-start(bf16[16,768]{1,0:T(8,128)(2,1)S(1)} %get-tuple-element.32), channel_id=1, source_target_pairs={{0,8},{8,16},{16,24},{24,32},{32,40},{40,48},{48,56},{56,64},{64,7... | collective-permute-start | bytes 73736 | tf_op jit(solution)/shard_map/ppermute | solution.py:21
  19.8 8.8 %collective-permute-start.3 = (bf16[16,768]{1,0:T(8,128)(2,1)S(1)}, bf16[16,768]{1,0:T(8,128)(2,1)S(1)}, u32[]{:S(2)}, u32[]{:S(2)}) collective-permute-start(bf16[16,768]{1,0:T(8,128)(2,1)S(1)} %get-tuple-element.33), channel_id=1, source_target_pairs={{8,0},{16,8},{24,16},{32,24},{40,32},{48,40},{56,48},{64,56},{72,6... | collective-permute-start | bytes 73736 | tf_op jit(solution)/shard_map/ppermute | solution.py:23
  29.7 9.6 %collective-permute-start.4 = (bf16[64,768]{1,0:T(8,128)(2,1)S(1)}, bf16[64,768]{1,0:T(8,128)(2,1)S(1)}, u32[]{:S(2)}, u32[]{:S(2)}) collective-permute-start(bf16[64,768]{1,0:T(8,128)(2,1)S(1)} %get-tuple-element.30), channel_id=1, source_target_pairs={{0,8},{8,16},{16,24},{24,32},{32,40},{40,48},{48,56},{56,64},{64,7... | collective-permute-start | bytes 294920 | tf_op jit(solution)/shard_map/ppermute | solution.py:21
  31.6 9.5 %collective-permute-start.5 = (bf16[64,768]{1,0:T(8,128)(2,1)S(1)}, bf16[64,768]{1,0:T(8,128)(2,1)S(1)}, u32[]{:S(2)}, u32[]{:S(2)}) collective-permute-start(bf16[64,768]{1,0:T(8,128)(2,1)S(1)} %get-tuple-element.31), channel_id=1, source_target_pairs={{8,0},{16,8},{24,16},{32,24},{40,32},{48,40},{56,48},{64,56},{72,6... | collective-permute-start | bytes 294920 | tf_op jit(solution)/shard_map/ppermute | solution.py:23
  42.9 8.4 %copy-start.4 = (bf16[768,128]{1,0:T(8,128)(2,1)S(1)}, bf16[768,128]{1,0:T(8,128)(2,1)}, u32[]{:S(2)}) copy-start(bf16[768,128]{1,0:T(8,128)(2,1)} %param.13) | copy-start | bytes 589828
  42.9 30.7 %copy-start.3 = (bf16[768,128]{1,0:T(8,128)(2,1)S(1)}, bf16[768,128]{1,0:T(8,128)(2,1)}, u32[]{:S(2)}) copy-start(bf16[768,128]{1,0:T(8,128)(2,1)} %param.14) | copy-start | bytes 589828
  43.8 29.8 %all-to-all-start = ((bf16[32,16,768]{2,1,0:T(8,128)(2,1)}), bf16[32,16,768]{2,1,0:T(8,128)(2,1)S(1)}, u32[]{:S(2)}, u32[]{:S(2)}) async-start(bf16[32,16,768]{2,1,0:T(8,128)(2,1)} %stack.2), calls=%async_computation | async-start | bytes 1572864 | tf_op jit(solution)/shard_map/all_to_all | solution.py:98
  74.5 9.9 %collective-permute-start.6 = (bf16[1,512,128]{2,1,0:T(8,128)(2,1)S(1)}, bf16[1,512,128]{2,1,0:T(8,128)(2,1)S(1)}, u32[]{:S(2)}, u32[]{:S(2)}) collective-permute-start(bf16[1,512,128]{2,1,0:T(8,128)(2,1)S(1)} %get-tuple-element.28), channel_id=1, source_target_pairs={{0,8},{8,16},{16,24},{24,32},{32,40},{40,48},{48,56},{56,64},{64,7... | collective-permute-start | bytes 393224 | tf_op jit(solution)/shard_map/ppermute | solution.py:21
  76.4 9.8 %collective-permute-start.7 = (bf16[1,512,128]{2,1,0:T(8,128)(2,1)S(1)}, bf16[1,512,128]{2,1,0:T(8,128)(2,1)S(1)}, u32[]{:S(2)}, u32[]{:S(2)}) collective-permute-start(bf16[1,512,128]{2,1,0:T(8,128)(2,1)S(1)} %get-tuple-element.29), channel_id=1, source_target_pairs={{8,0},{16,8},{24,16},{32,24},{40,32},{48,40},{56,48},{64,56},{72,6... | collective-permute-start | bytes 393224 | tf_op jit(solution)/shard_map/ppermute | solution.py:23
  87.6 3.8 %copy-start.2 = (bf16[3,3,128,128]{3,2,1,0:T(8,128)(2,1)S(1)}, bf16[3,3,128,128]{3,2,1,0:T(8,128)(2,1)}, u32[]{:S(2)}) copy-start(bf16[3,3,128,128]{3,2,1,0:T(8,128)(2,1)} %param.15) | copy-start | bytes 884740
  97.3 3.3 %copy-start.1 = (bf16[512,768]{1,0:T(8,128)(2,1)S(1)}, bf16[512,768]{1,0:T(8,128)(2,1)}, u32[]{:S(2)}) copy-start(bf16[512,768]{1,0:T(8,128)(2,1)} %param.9) | copy-start | bytes 2359300
